TPU v7x, 32 devices: a whole 2x2x4 slice. The times are simulated.
32 devices in a mesh: ffn: 16 (over z, y, core), tok: 2 (over x).
Axes of the slice: x: 2, y: 2, z: 4, core: 2. Of those that a mesh axis runs over, the one named last changes fastest.
Arguments:
- tokens: bfloat16 [16384, 768], P(('ffn', 'tok')), may hold values from -6 to 6
- joint_proj: bfloat16 [768, 2304], replicated, may hold values from -0.21875 to 0.21875
- query_bias: bfloat16 [768], replicated, may hold values from -1.5 to 1.5
- value_bias: bfloat16 [768], replicated, may hold values from -1.5 to 1.5
- out_proj: bfloat16 [768, 768], replicated, may hold values from -1.75 to 1.75
- out_bias: bfloat16 [768], replicated, may hold values from -1.5 to 1.5
- first_gain: float32 [768], replicated, may hold values from 0.5 to 1.5
- first_shift: float32 [768], replicated, may hold values from -1.5 to 1.5
- inner_proj: bfloat16 [768, 3072], P(None, 'ffn'), may hold values from -0.21875 to 0.21875
- inner_bias: bfloat16 [3072], P('ffn'), may hold values from -1.5 to 1.5
- outer_proj: bfloat16 [3072, 768], P('ffn'), may hold values from -0.15625 to 0.15625
- outer_bias: bfloat16 [768], replicated, may hold values from -1.5 to 1.5
- second_gain: float32 [768], replicated, may hold values from 0.5 to 1.5
- second_shift: float32 [768], replicated, may hold values from -1.5 to 1.5
- segment_ids: int32 [16384], P(('ffn', 'tok')), may hold values from 0 to 3, as said below
- cls_positions: int32 [32, 4], P(('ffn', 'tok')), may hold values from 0 to 480, as said below
- widths: int32 [2, 2], replicated, may hold values from 3 to 3072, as said below
- out_grad: bfloat16 [16384, 768], P(('ffn', 'tok')), may hold values from -6 to 6
Outputs:
- output: bfloat16 [16384, 768], P(('ffn', 'tok'))
- cls_states: float32 [32, 4, 768], P(('ffn', 'tok'))
- input_grad: float32 [16384, 768], P(('ffn', 'tok'))
- joint_proj_grad: float32 [768, 2304], replicated
- query_bias_grad: float32 [768], replicated
- value_bias_grad: float32 [768], replicated
- out_proj_grad: float32 [768, 768], replicated
- out_bias_grad: float32 [768], replicated
- first_gain_grad: float32 [768], replicated
- first_shift_grad: float32 [768], replicated
- inner_proj_grad: float32 [768, 3072], P(None, 'ffn')
- inner_bias_grad: float32 [3072], P('ffn')
- outer_proj_grad: float32 [3072, 768], P('ffn')
- outer_bias_grad: float32 [768], replicated
- second_gain_grad: float32 [768], replicated
- second_shift_grad: float32 [768], replicated
Inputs may be any that keep to these rules, and one draw needn't show every extreme that they name: `segment_ids`: each row of 512 tokens holds exactly 4 examples numbered 0 to 3 in order, each of one token or more. `cls_positions`: the first position of each example of a row, counted from the row's start, in the order of the examples; the first is 0; the last example's start reaches the most in some row. `widths`: row m: neurons kept (a multiple of 768, at least 768) and heads kept (a multiple of 3, at least 3) of micro-batch m; one micro-batch keeps all 3072 neurons and all 12 heads.
All inputs are finite; a program needn't handle non-finite values.
Results may differ from a plain program's by a relative error of at most 0.014.
The roundings to bfloat16 on the way count: a program that leaves them out, or rounds other values in their place, can miss the bound.
Values may be sent and summed in bfloat16 or wider, within the bound.
A program may use at most 256 MiB of HBM per device.

v0:
```python
import math
import jax
import jax.numpy as jnp
from jax import lax
from jax.sharding import PartitionSpec as P

HEADS = 12
DH = 64
MB = 2


def normalize(inputs, gain_vec, shift_vec):
    row_mean = jnp.mean(inputs, axis=-1, keepdims=True)
    centred = inputs - row_mean
    row_scale = lax.rsqrt(jnp.mean(centred * centred, axis=-1, keepdims=True) + 1e-12)
    normed = centred * row_scale
    return (normed * gain_vec + shift_vec, normed, row_scale)


def normalize_back(incoming, normed, row_scale, gain_vec):
    gain_grad = jnp.sum(incoming * normed, axis=0)
    shift_grad = jnp.sum(incoming, axis=0)
    scaled_grad = incoming * gain_vec
    inputs_grad = row_scale * (
        scaled_grad
        - jnp.mean(scaled_grad, axis=-1, keepdims=True)
        - normed * jnp.mean(scaled_grad * normed, axis=-1, keepdims=True)
    )
    return (inputs_grad, gain_grad, shift_grad)


def gelu_slope(inputs):
    return (
        0.5 * (1.0 + lax.erf(inputs * 0.7071067811865476))
        + inputs * jnp.exp(-0.5 * inputs * inputs) * 0.3989422804014327
    )


def contract_rows(left_side, right_side):
    return lax.dot_general(
        left_side, right_side, (((0,), (0,)), ((), ())), preferred_element_type=jnp.float32
    )


def contract_cols(left_side, right_side):
    return lax.dot_general(
        left_side, right_side, (((1,), (1,)), ((), ())), preferred_element_type=jnp.float32
    )


def on_device(
    tokens,
    joint_proj,
    query_bias,
    value_bias,
    out_proj,
    out_bias,
    first_gain,
    first_shift,
    inner_proj,
    inner_bias,
    outer_proj,
    outer_bias,
    second_gain,
    second_shift,
    segment_ids,
    cls_positions,
    widths,
    out_grad,
):
    tok_rows, model_width = tokens.shape
    seq_rows = cls_positions.shape[0]
    seq_len = tok_rows // seq_rows
    unit_share = inner_proj.shape[1]
    ffn_count = lax.axis_size("ffn")
    tok_count = lax.axis_size("tok")
    ffn_place = lax.axis_index("ffn")
    tok_place = lax.axis_index("tok")
    per_group = seq_rows * ffn_count * tok_count // MB
    batches = jnp.arange(MB, dtype=jnp.int32)
    own_group = (ffn_place * tok_count + tok_place) * seq_rows // per_group
    own_pick = (batches == own_group).astype(jnp.int32)
    heads_kept = jnp.sum(own_pick * widths[:, 1])
    head_on = (jnp.arange(HEADS, dtype=jnp.int32) < heads_kept).astype(jnp.float32)
    factor = 1.0 / math.sqrt(DH)
    zero_bias = jnp.zeros((model_width,), jnp.bfloat16)
    joint_bias = jnp.concatenate([query_bias, zero_bias, value_bias])
    joint_low = (
        jnp.dot(tokens, joint_proj, preferred_element_type=jnp.float32) + joint_bias
    ).astype(jnp.bfloat16)
    joint_low = joint_low.reshape(seq_rows, seq_len, 3, HEADS, DH)
    queries = joint_low[:, :, 0]
    key_heads = joint_low[:, :, 1]
    value_heads = joint_low[:, :, 2]
    segments = segment_ids.reshape(seq_rows, seq_len)
    same_doc = (segments[:, :, None] == segments[:, None, :])[:, None]

    def scores_of(query_rows, key_rows):
        raw_scores = (
            jnp.einsum("rqhd,rkhd->rhqk", query_rows, key_rows, preferred_element_type=jnp.float32)
            * factor
        )
        return jnp.where(same_doc, raw_scores, -1e30)

    scores = scores_of(queries, key_heads)
    row_peak = jnp.max(scores, axis=-1, keepdims=True)
    log_total = row_peak + jnp.log(jnp.sum(jnp.exp(scores - row_peak), axis=-1, keepdims=True))
    probs_low = jnp.exp(scores - log_total).astype(jnp.bfloat16)
    context = (
        jnp.einsum("rhqk,rkhd->rqhd", probs_low, value_heads, preferred_element_type=jnp.float32)
        * head_on[:, None]
    )
    context_low = context.astype(jnp.bfloat16).reshape(tok_rows, model_width)
    attn_out = jnp.dot(context_low, out_proj, preferred_element_type=jnp.float32) + out_bias
    first_out, first_normed, first_scale = normalize(
        tokens.astype(jnp.float32) + attn_out, first_gain, first_shift
    )
    first_low = first_out.astype(jnp.bfloat16)
    unit_total = unit_share * ffn_count
    stacked = lax.all_gather(jnp.stack([inner_proj.T, outer_proj]), "ffn", axis=1, tiled=True)
    inner_rows, outer_rows = (stacked[0], stacked[1])
    inner_bias_all = lax.all_gather(inner_bias, "ffn", axis=0, tiled=True)
    own_kept = jnp.sum(own_pick * widths[:, 0])
    neuron_on = (jnp.arange(unit_total, dtype=jnp.int32) < own_kept).astype(jnp.float32)
    pre_act = contract_cols(first_low, inner_rows) + inner_bias_all
    act_low = (jax.nn.gelu(pre_act, approximate=False) * neuron_on).astype(jnp.bfloat16)
    ffn_out = jnp.dot(act_low, outer_rows, preferred_element_type=jnp.float32) + outer_bias
    second_out, second_normed, second_scale = normalize(
        first_out + ffn_out, second_gain, second_shift
    )
    output = second_out.astype(jnp.bfloat16)
    cls_states = jnp.take_along_axis(
        second_out.reshape(seq_rows, seq_len, model_width), cls_positions[:, :, None], axis=1
    )
    sum_grad, second_gain_grad, second_shift_grad = normalize_back(
        out_grad.astype(jnp.float32), second_normed, second_scale, second_gain
    )
    ffn_grad = sum_grad.astype(jnp.bfloat16)
    outer_bias_grad = jnp.sum(ffn_grad.astype(jnp.float32), axis=0)
    outer_proj_grad = contract_rows(act_low, ffn_grad)
    act_grad = contract_cols(ffn_grad, outer_rows)
    pre_grad = (act_grad * (gelu_slope(pre_act) * neuron_on)).astype(jnp.bfloat16)
    inner_bias_sum = jnp.sum(pre_grad.astype(jnp.float32), axis=0)
    inner_rows_grad = contract_rows(pre_grad, first_low)
    first_back = jnp.dot(pre_grad, inner_rows, preferred_element_type=jnp.float32)
    unit_grads = jnp.stack(
        [inner_rows_grad.astype(jnp.bfloat16), outer_proj_grad.astype(jnp.bfloat16)]
    )
    unit_grads = lax.psum_scatter(unit_grads, "ffn", scatter_dimension=1, tiled=True)
    unit_grads = lax.psum(unit_grads, "tok").astype(jnp.float32)
    inner_proj_grad, outer_proj_grad = (unit_grads[0].T, unit_grads[1])
    first_grad = sum_grad + first_back
    attn_sum_grad, first_gain_grad, first_shift_grad = normalize_back(
        first_grad, first_normed, first_scale, first_gain
    )
    attn_grad = attn_sum_grad.astype(jnp.bfloat16)
    out_bias_grad = jnp.sum(attn_grad.astype(jnp.float32), axis=0)
    out_proj_grad = contract_rows(context_low, attn_grad)
    context_grad = (
        contract_cols(attn_grad, out_proj)
        .astype(jnp.bfloat16)
        .reshape(seq_rows, seq_len, HEADS, DH)
    )
    context_grad = context_grad * head_on.astype(jnp.bfloat16)[:, None]
    scores = scores_of(queries, key_heads)
    probs = jnp.exp(scores - log_total)
    probs_again = probs.astype(jnp.bfloat16)
    value_part = jnp.einsum(
        "rhqk,rqhd->rkhd", probs_again, context_grad, preferred_element_type=jnp.float32
    )
    prob_grad = jnp.einsum(
        "rqhd,rkhd->rhqk", context_grad, value_heads, preferred_element_type=jnp.float32
    )
    score_grad = (probs * (prob_grad - jnp.sum(probs * prob_grad, axis=-1, keepdims=True))).astype(
        jnp.bfloat16
    )
    query_part = (
        jnp.einsum("rhqk,rkhd->rqhd", score_grad, key_heads, preferred_element_type=jnp.float32)
        * factor
    )
    key_part = (
        jnp.einsum("rhqk,rqhd->rkhd", score_grad, queries, preferred_element_type=jnp.float32)
        * factor
    )
    joint_grad = (
        jnp.stack([query_part, key_part, value_part], axis=2)
        .astype(jnp.bfloat16)
        .reshape(tok_rows, 3 * model_width)
    )
    joint_bias_grad = jnp.sum(joint_grad.astype(jnp.float32), axis=0)
    query_bias_grad = joint_bias_grad[:model_width]
    value_bias_grad = joint_bias_grad[2 * model_width :]
    joint_proj_grad = contract_rows(tokens, joint_grad)
    input_grad = attn_sum_grad + contract_cols(joint_grad, joint_proj)
    joint_proj_grad, out_proj_grad = lax.psum(
        (joint_proj_grad.astype(jnp.bfloat16), out_proj_grad.astype(jnp.bfloat16)), ("ffn", "tok")
    )
    joint_proj_grad = joint_proj_grad.astype(jnp.float32)
    out_proj_grad = out_proj_grad.astype(jnp.float32)
    small = [
        query_bias_grad,
        value_bias_grad,
        out_bias_grad,
        first_gain_grad,
        first_shift_grad,
        outer_bias_grad,
        second_gain_grad,
        second_shift_grad,
        inner_bias_sum,
    ]
    small = lax.psum(jnp.concatenate(small), ("ffn", "tok"))
    (
        query_bias_grad,
        value_bias_grad,
        out_bias_grad,
        first_gain_grad,
        first_shift_grad,
        outer_bias_grad,
        second_gain_grad,
        second_shift_grad,
    ) = [small[i * model_width : (i + 1) * model_width] for i in range(8)]
    inner_bias_grad = lax.dynamic_slice(
        small, (8 * model_width + ffn_place * unit_share,), (unit_share,)
    )
    return (
        output,
        cls_states,
        input_grad,
        joint_proj_grad,
        query_bias_grad,
        value_bias_grad,
        out_proj_grad,
        out_bias_grad,
        first_gain_grad,
        first_shift_grad,
        inner_proj_grad,
        inner_bias_grad,
        outer_proj_grad,
        outer_bias_grad,
        second_gain_grad,
        second_shift_grad,
    )


def solution(mesh):
    return jax.shard_map(
        on_device,
        mesh=mesh,
        in_specs=(
            P(("ffn", "tok"), None),
            P(),
            P(),
            P(),
            P(),
            P(),
            P(),
            P(),
            P(None, "ffn"),
            P("ffn"),
            P("ffn", None),
            P(),
            P(),
            P(),
            P(("ffn", "tok")),
            P(("ffn", "tok"), None),
            P(),
            P(("ffn", "tok"), None),
        ),
        out_specs=(
            P(("ffn", "tok"), None),
            P(("ffn", "tok"), None, None),
            P(("ffn", "tok"), None),
            P(),
            P(),
            P(),
            P(),
            P(),
            P(),
            P(),
            P(None, "ffn"),
            P("ffn"),
            P("ffn", None),
            P(),
            P(),
            P(),
        ),
        check_vma=False,
    )
```

profile of v0, /device:TPU:0, one launch (start us, length us, event | category | flops | bytes accessed | tf_op | source)
XLA Modules:
  0.0 448.7 jit_solution(7823230462201781648)
XLA Ops:
  14.7 37.2 %all-reduce = bf16[3072]{0:T(1024)(128)(2,1)S(1)} all-reduce(bf16[3072]{0:T(1024)(128)(2,1)S(1)} %dynamic-update-slice), channel_id=1, replica_groups=mesh['ffn'=16,'tok'=2] {'ffn'}, use_global_device_ids=true, to_apply=%add | all-reduce | flops 3072 | bytes 12288
  53.2 4.5 %fusion.22 = bf16[512,2304]{1,0:T(8,128)(2,1)} fusion(bf16[512,768]{1,0:T(8,128)(2,1)} %param.18, bf16[768,2304]{1,0:T(8,128)(2,1)S(1)} %copy-done, f32[2304]{0:T(1024)S(1)} %maximum_convert_fusion.1), kind=kOutput, calls=%fused_computation.48 | convolution fusion | flops 1814298624 | bytes 6693888 | tf_op jit(solution)/shard_map/dot_general | solution.py:89
  57.7 4.3 copy.43
  66.2 3.5 fusion
  69.7 3.7 exponential_reduce_fusion
  74.3 4.8 %fusion.34 = bf16[1,12,64,512]{3,2,1,0:T(8,128)(2,1)S(1)} fusion(f32[12]{0:T(128)S(1)} %get-tuple-element.95, bf16[1,512,3,12,64]{1,4,3,2,0:T(8,128)(2,1)} %bitcast.110, f32[12,512,512]{1,2,0:T(8,128)S(1)} %get-tuple-element.83, f32[12,512]{1,0:T(8,128)S(1)} %log_add_fusion, pred[512,512]{0,1:T(8,128)(4,1)} %copy-done.3), kind=kOutput, calls=%fused_computation.64 | convolution fusion | flops 416022528 | bytes 14442544 | tf_op jit(solution)/shard_map/rhqk,rkhd->rqhd/dot_general | solution.py:110
  82.1 13.0 %all-gather.2.cloned.1.call-done = bf16[2,3072,768]{2,1,0:T(8,128)(2,1)} async-done(((bf16[2,192,768]{2,1,0:T(8,128)(2,1)}), bf16[2,3072,768]{2,1,0:T(8,128)(2,1)}) %all-gather.2.cloned.1.call-update) | async-done | bytes 9437200 | tf_op jit(solution)/shard_map/all_gather | solution.py:120
  95.1 18.9 %fusion.5 = (bf16[512,3072]{1,0:T(8,128)(2,1)S(1)}, f32[512,3072]{1,0:T(8,128)S(1)}) fusion(f32[3072]{0:T(1024)} %fusion.45, f32[3072]{0:T(1024)S(1)} %copy-done.19, bf16[2,3072,768]{2,1,0:T(8,128)(2,1)} %all-gather.2.cloned.1.call-done, f32[512,768]{1,0:T(8,128)} %copy-done.7, f32[768]{0:T(1024)} %param.25, f32[768]{0:T(1024)} %param.24, ...), kind=kOutput, calls=%fused_computation.14 | convolution fusion | flops 2523267072 | bytes 15765504 | tf_op jit(solution)/shard_map/dot_general | solution.py:46
  114.1 2.8 fusion.65
  121.2 4.4 fusion.21
  125.5 6.3 %convert_reduce_fusion = (f32[3072]{0:T(1024)}, bf16[512,3072]{1,0:T(8,128)(2,1)S(1)}) fusion(f32[3072]{0:T(1024)S(1)} %copy-done.20, f32[512,3072]{1,0:T(8,128)S(1)} %get-tuple-element.87, f32[3072]{0:T(1024)S(1)} %copy-done.19, bf16[2,3072,768]{2,1,0:T(8,128)(2,1)S(1)} %copy-done.31, f32[512,768]{1,0:T(8,128)S(1)} %get-tuple-element.61), kind=kOutput, calls=%fused_computation.22 | convolution fusion | flops 2438329344 | bytes 15765504 | tf_op jit(solution)/shard_map/dot_general | solution.py:46
  133.5 5.0 %fusion.20 = bf16[1,3072,768]{2,1,0:T(8,128)(2,1)} fusion(bf16[512,3072]{1,0:T(8,128)(2,1)S(1)} %get-tuple-element.94, f32[512,768]{1,0:T(8,128)S(1)} %copy-done.8, f32[768]{0:T(1024)S(1)} %copy-done.36, f32[768]{0:T(1024)S(1)} %copy-done.24, f32[512]{0:T(512)S(1)} %copy-done.22, f32[512]{0:T(512)S(1)} %broadcast_multiply_fusion.5), kind=kOutput, calls=%fused_computation.46 | convolution fusion | flops 2420244480 | bytes 9447424 | tf_op jit(solution)/shard_map/dot_general | solution.py:40
  138.6 8.2 %pad_maximum_fusion = bf16[2,3072,768]{2,1,0:T(8,128)(2,1)} fusion(bf16[1,3072,768]{2,1,0:T(8,128)(2,1)} %fusion.21, bf16[1,3072,768]{2,1,0:T(8,128)(2,1)} %fusion.20), kind=kLoop, calls=%fused_computation.9 | loop fusion | flops 4718592 | bytes 18874368 | tf_op jit(solution)/shard_map/stack | solution.py:146
  147.5 8.3 %multiply_reduce_fusion.1 = (f32[768]{0:T(1024)}, f32[512]{0:T(512)S(1)}, f32[512]{0:T(512)S(1)}, f32[768]{0:T(1024)}, f32[512,768]{1,0:T(8,128)S(1)}) fusion(f32[512,768]{1,0:T(8,128)} %copy-done.7, f32[512]{0:T(512)S(1)} %copy-done.23, f32[512]{0:T(512)S(1)} %broadcast_multiply_fusion.5, f32[768]{0:T(1024)S(1)} %copy-done.25, f32[512,768]{1,0:T(8,128)} %copy-done.13, ...), kind=kOutput, calls=%fused_computation.66 | convolution fusion | flops 2419848704 | bytes 12600320 | tf_op jit(solution)/shard_map/dot_general | solution.py:145
  162.2 14.8 %multiply_reduce_fusion = (f32[12,512]{1,0:T(8,128)S(1)}, f32[12,512,512]{1,2,0:T(8,128)}) fusion(f32[12,512,512]{1,2,0:T(8,128)} %copy-done.1, f32[12,512]{1,0:T(8,128)} %copy-done.16, pred[512,512]{0,1:T(8,128)(4,1)} %copy-done.3, bf16[1,512,3,12,64]{1,4,3,2,0:T(8,128)(2,1)} %bitcast.111, bf16[512,12,64]{0,2,1:T(8,128)(2,1)} %bitcast.114, ...), kind=kOutput, calls=%fused_computation.2 | convolution fusion | flops 418768896 | bytes 27058200 | tf_op jit(solution)/shard_map/rqhd,rkhd->rhqk/dot_general | solution.py:171
  177.1 7.7 %multiply_convert_fusion = bf16[12,512,512]{1,2,0:T(8,128)(2,1)S(1)} fusion(f32[12,512,512]{1,2,0:T(8,128)} %get-tuple-element.92, f32[12,512,512]{1,2,0:T(8,128)S(1)} %bitcast.108, f32[12,512]{1,0:T(8,128)S(1)} %get-tuple-element.91, f32[12,512]{1,0:T(8,128)S(1)} %copy-done.17, pred[512,512]{0,1:T(8,128)(4,1)S(1)} %copy-done.4), kind=kLoop, calls=%fused_computation.1 | loop fusion | flops 18874368 | bytes 31768576 | tf_op jit(solution)/shard_map/convert_element_type | solution.py:174
  188.0 3.7 convolution_bitcast_fusion
  195.1 3.8 fusion.23
  216.0 41.3 %psum.29 = f32[9216]{0:T(1024)} all-reduce(f32[9216]{0:T(1024)} %constant_dynamic-update-slice_fusion), channel_id=1, replica_groups=mesh['ffn'=16,'tok'=2] {'ffn','tok'}, use_global_device_ids=true, to_apply=%region_22.23 | all-reduce | flops 9216 | bytes 73728 | tf_op jit(solution)/shard_map/psum | solution.py:211
  261.4 5.3 %convolution_add_fusion.1 = f32[512,768]{1,0:T(8,128)} fusion(f32[512,768]{1,0:T(8,128)} %copy-done.5, bf16[512,2304]{0,1:T(8,128)(2,1)} %bitcast.117, bf16[768,2304]{1,0:T(8,128)(2,1)S(1)} %copy-done), kind=kOutput, calls=%fused_computation.83 | convolution fusion | flops 1812332544 | bytes 9043968 | tf_op jit(solution)/shard_map/dot_general | solution.py:46
  266.7 142.0 %all-reduce.7.cloned.1.call-done = (bf16[768,2304]{0,1:T(8,128)(2,1)}, bf16[768,768]{1,0:T(8,128)(2,1)}) async-done(((bf16[768,2304]{0,1:T(8,128)(2,1)}, bf16[768,768]{1,0:T(8,128)(2,1)}), (bf16[768,2304]{0,1:T(8,128)(2,1)}, bf16[768,768]{1,0:T(8,128)(2,1)})) %all-reduce.7.cloned.1.call-update) | async-done | bytes 4718608 | tf_op jit(solution)/shard_map/psum | solution.py:195
  408.7 2.8 convert_element_type.176
  411.5 5.9 %copy.49 = f32[768,2304]{1,0:T(8,128)} copy(bf16[768,2304]{0,1:T(8,128)(2,1)} %get-tuple-element.58) | data formatting | bytes 10616832
  417.5 22.3 %all-reduce.5.cloned.1.call-done = bf16[2,192,768]{2,1,0:T(8,128)(2,1)} async-done(((bf16[2,192,768]{2,1,0:T(8,128)(2,1)}), bf16[2,192,768]{2,1,0:T(8,128)(2,1)}) %all-reduce.5.cloned.1.call-update) | async-done | bytes 589840 | tf_op jit(solution)/shard_map/psum | solution.py:150
  (152 shorter events, 59.0 us)
Async XLA Ops:
  7.2 46.0 %copy-start = (bf16[768,2304]{1,0:T(8,128)(2,1)S(1)}, bf16[768,2304]{1,0:T(8,128)(2,1)}, u32[]{:S(2)}) copy-start(bf16[768,2304]{1,0:T(8,128)(2,1)} %param.19) | copy-start | bytes 10616836
  7.2 87.9 %all-gather.2.cloned.1.call-start = ((), (), s32[]{:S(2)}) async-start(), calls=%async_computation.1 | async-start | bytes 10027008 | tf_op jit(solution)/shard_map/all_gather | solution.py:120
  9.3 252.0 %reduce-scatter.2.cloned.1.call-start = ((), (), s32[]{:S(2)}) async-start(), calls=%async_computation.2 | async-start | bytes 10027008 | tf_op jit(solution)/shard_map/reduce_scatter | solution.py:149
  57.7 8.2 %copy-start.21 = (s32[512]{0:T(512)S(1)}, s32[512]{0:T(512)}, u32[]{:S(2)}) copy-start(s32[512]{0:T(512)} %param.32) | copy-start | bytes 6148
  73.4 5.6 %copy-start.16 = (f32[12,512]{1,0:T(8,128)}, f32[12,512]{1,0:T(8,128)S(1)}, u32[]{:S(2)}) copy-start(f32[12,512]{1,0:T(8,128)S(1)} %log_add_fusion) | copy-start | bytes 73732
  74.3 4.8 %copy-start.32 = (bf16[768,768]{1,0:T(8,128)(2,1)S(1)}, bf16[768,768]{1,0:T(8,128)(2,1)}, u32[]{:S(2)}) copy-start(bf16[768,768]{1,0:T(8,128)(2,1)} %param.22) | copy-start | bytes 3538948
  74.3 4.8 %copy-start.34 = (bf16[512,768]{1,0:T(8,128)(2,1)S(1)}, bf16[512,768]{1,0:T(8,128)(2,1)}, u32[]{:S(2)}) copy-start(bf16[512,768]{1,0:T(8,128)(2,1)} %param.18) | copy-start | bytes 2359300
  79.1 16.0 %copy-start.19 = (f32[3072]{0:T(1024)S(1)}, f32[3072]{0:T(1024)}, u32[]{:S(2)}) copy-start(f32[3072]{0:T(1024)} %convert_element_type.154) | copy-start | bytes 36868
  95.1 18.9 %copy-start.8 = (f32[512,768]{1,0:T(8,128)S(1)}, f32[512,768]{1,0:T(8,128)}, u32[]{:S(2)}) copy-start(f32[512,768]{1,0:T(8,128)} %copy-done.7) | copy-start | bytes 4718596
  95.1 18.9 %copy-start.22 = (f32[512]{0:T(512)S(1)}, f32[512]{0:T(512)}, u32[]{:S(2)}) copy-start(f32[512]{0:T(512)} %add_rsqrt_fusion.1) | copy-start | bytes 6148
  95.1 18.9 %copy-start.24 = (f32[768]{0:T(1024)S(1)}, f32[768]{0:T(1024)}, u32[]{:S(2)}) copy-start(f32[768]{0:T(1024)} %param.24) | copy-start | bytes 9220
  95.1 18.9 %copy-start.26 = (f32[768]{0:T(1024)S(1)}, f32[768]{0:T(1024)}, u32[]{:S(2)}) copy-start(f32[768]{0:T(1024)} %convert_element_type.157) | copy-start | bytes 9220
  95.1 18.9 %copy-start.31 = (bf16[2,3072,768]{2,1,0:T(8,128)(2,1)S(1)}, bf16[2,3072,768]{2,1,0:T(8,128)(2,1)}, u32[]{:S(2)}) copy-start(bf16[2,3072,768]{2,1,0:T(8,128)(2,1)} %all-gather.2.cloned.1.call-done) | copy-start | bytes 28311556
  95.1 18.9 %copy-start.36 = (f32[768]{0:T(1024)S(1)}, f32[768]{0:T(1024)}, u32[]{:S(2)}) copy-start(f32[768]{0:T(1024)} %param.25) | copy-start | bytes 9220
  146.8 261.9 %all-reduce.7.cloned.1.call-start = ((), (), s32[]{:S(2)}) async-start(), calls=%async_computation.4 | async-start | bytes 9437184 | tf_op jit(solution)/shard_map/psum | solution.py:195
  147.5 8.3 %copy-start.9 = (f32[512,768]{1,0:T(8,128)S(1)}, f32[512,768]{1,0:T(8,128)}, u32[]{:S(2)}) copy-start(f32[512,768]{1,0:T(8,128)} %copy-done.7) | copy-start | bytes 4718596
  155.8 6.4 %copy-start.30 = (bf16[12]{0:T(256)(128)(2,1)S(1)}, bf16[12]{0:T(256)(128)(2,1)}, u32[]{:S(2)}) copy-start(bf16[12]{0:T(256)(128)(2,1)} %get-tuple-element.96) | copy-start | bytes 76
  162.1 14.9 %slice-start = ((s8[12582912]{0:T(1024)(128)(4,1)}), s8[4194304]{0:T(1024)(128)(4,1)S(1)}, s32[]{:S(2)}) async-start(s8[12582912]{0:T(1024)(128)(4,1)} %bitcast.107), calls=%async_computation.5 | async-start | bytes 8388608
  162.1 14.9 %slice-start.1 = ((s8[12582912]{0:T(1024)(128)(4,1)}), s8[4194304]{0:T(1024)(128)(4,1)S(1)}, s32[]{:S(2)}) async-start(s8[12582912]{0:T(1024)(128)(4,1)} %bitcast.107), calls=%async_computation.6 | async-start | bytes 8388608
  162.1 14.9 %slice-start.2 = ((s8[12582912]{0:T(1024)(128)(4,1)}), s8[4194304]{0:T(1024)(128)(4,1)S(1)}, s32[]{:S(2)}) async-start(s8[12582912]{0:T(1024)(128)(4,1)} %bitcast.107), calls=%async_computation.7 | async-start | bytes 8388608
  162.1 14.9 %copy-start.4 = (pred[512,512]{0,1:T(8,128)(4,1)S(1)}, pred[512,512]{0,1:T(8,128)(4,1)}, u32[]{:S(2)}) copy-start(pred[512,512]{0,1:T(8,128)(4,1)} %copy-done.3) | copy-start | bytes 786436
  162.2 14.9 %copy-start.17 = (f32[12,512]{1,0:T(8,128)S(1)}, f32[12,512]{1,0:T(8,128)}, u32[]{:S(2)}) copy-start(f32[12,512]{1,0:T(8,128)} %copy-done.16) | copy-start | bytes 73732
  177.0 7.8 %copy-start.2 = (bf16[512,2304]{0,1:T(8,128)(2,1)S(1)}, bf16[512,2304]{0,1:T(8,128)(2,1)}, u32[]{:S(2)}) copy-start(bf16[512,2304]{0,1:T(8,128)(2,1)} %copy.43) | copy-start | bytes 7077892
  198.9 240.8 %all-reduce.5.cloned.1.call-start = ((), (), s32[]{:S(2)}) async-start(), calls=%async_computation.3 | async-start | bytes 1179648 | tf_op jit(solution)/shard_map/psum | solution.py:150
  (22 other events, 56.8 us)
Sparse Core Ops, SparseCore 0:
  10.9 84.1 all-gather.1
  146.9 110.6 reduce-scatter.1
  264.0 144.5 all-reduce.6
  410.8 28.8 all-reduce.4
where the time goes:
time: 457 us; the launch traced here: 449 us
  waiting for transfers between devices  177 us (39%)
  matrix products  93.7 us (21%)
  blocking collectives  78.5 us (17%)
  other arithmetic  43.2 us (9%)
  local copies, waits for them, and re-layouts  40.8 us (9%)
  between operations  15.1 us (3%)
    psum x1, waiting for transfers between devices, on_device(): lax.psum((joint_proj_grad.astype(jnp.bfloat16), out_proj_grad.astype(jnp....  142 us
    psum x1, blocking collectives, on_device(): small = lax.psum(jnp.concatenate(small), ('ffn', 'tok'))  41.3 us
    unnamed x1, blocking collectives  37.2 us
    dot_general x4, matrix products, contract_cols(): lax.dot_general(left_side, right_side, (((1,), (1,)), ((), ())), preferre...  32.2 us
    unnamed x96, local copies, waits for them, and re-layouts  25.2 us
    psum x1, waiting for transfers between devices, on_device(): unit_grads = lax.psum(unit_grads, 'tok').astype(jnp.float32)  22.3 us
    dot_general x4, matrix products, contract_rows(): lax.dot_general(left_side, right_side, (((0,), (0,)), ((), ())), preferre...  15 us
    dot_general x1, matrix products, on_device(): jnp.einsum('rqhd,rkhd->rhqk', context_grad, value_heads, preferred_elemen...  14.8 us
  transfers between devices with their start and end apart: 4, of which 3 were waited for; matrix products, arithmetic and copies ran while one was open for 26% of the time, Pallas kernels for 0%

commit v1 on v0

--- a/solution.py
+++ b/solution.py
@@ -7,6 +7,12 @@
 HEADS = 12
 DH = 64
 MB = 2
+
+
+def gather_and_add(array, name):
+    parts = lax.all_gather(array, name, axis=0, tiled=False)
+    total = parts.sum(axis=0)
+    return total
 
 
 def normalize(inputs, gain_vec, shift_vec):
@@ -208,7 +214,7 @@
         second_shift_grad,
         inner_bias_sum,
     ]
-    small = lax.psum(jnp.concatenate(small), ("ffn", "tok"))
+    small = gather_and_add(jnp.concatenate(small), ("ffn", "tok"))
     (
         query_bias_grad,
         value_bias_grad,

time: 457 us -> 512 us (1.12)
  waiting for transfers between devices: 177 us -> 267 us
  blocking collectives: 78.5 us -> 37.2 us
    all_gather x0 -> x1, waiting for transfers between devices: none -> 48.6 us  [gather_and_add(): parts = lax.all_gather(array, name, axis=0, tiled=False)]
    psum x1 -> x0, blocking collectives: 41.3 us -> none  [on_device(): small = lax.psum(jnp.concatenate(small), ('ffn', 'tok'))]
    reduce_scatter x1, waiting for transfers between devices: 0.01 us -> 40.1 us  [on_device(): lax.psum_scatter(unit_grads, 'ffn', scatter_dimension=1, tiled=True)]
    unnamed x96 -> x88, local copies, waits for them, and re-layouts: 25.2 us -> 24.6 us
  transfers between devices with their start and end apart: 4 -> 5, of which waited for: 3 -> 5; matrix products, arithmetic and copies ran while one was open for 26% -> 25% of each run, Pallas kernels for 0% -> 0%
where the time goes in v1:
time: 512 us; the launch traced here: 504 us
  waiting for transfers between devices  267 us (52%)
  matrix products  97.3 us (19%)
  other arithmetic  45.3 us (9%)
  local copies, waits for them, and re-layouts  41.8 us (8%)
  blocking collectives  37.2 us (7%)
  between operations  15.1 us (3%)
    psum x1, waiting for transfers between devices, on_device(): lax.psum((joint_proj_grad.astype(jnp.bfloat16), out_proj_grad.astype(jnp....  143 us
    all_gather x1, waiting for transfers between devices, gather_and_add(): parts = lax.all_gather(array, name, axis=0, tiled=False)  48.6 us
    reduce_scatter x1, waiting for transfers between devices, on_device(): lax.psum_scatter(unit_grads, 'ffn', scatter_dimension=1, tiled=True)  40.1 us
    unnamed x1, blocking collectives  37.2 us
    dot_general x4, matrix products, contract_cols(): lax.dot_general(left_side, right_side, (((1,), (1,)), ((), ())), preferre...  32.2 us
    unnamed x88, local copies, waits for them, and re-layouts  24.6 us
    psum x1, waiting for transfers between devices, on_device(): unit_grads = lax.psum(unit_grads, 'tok').astype(jnp.float32)  22.2 us
    dot_general x4, matrix products, contract_rows(): lax.dot_general(left_side, right_side, (((0,), (0,)), ((), ())), preferre...  18.6 us
  transfers between devices with their start and end apart: 5, of which 5 were waited for; matrix products, arithmetic and copies ran while one was open for 25% of the time, Pallas kernels for 0%

profile of v1, /device:TPU:0, one launch (start us, length us, event | category | flops | bytes accessed | tf_op | source)
XLA Modules:
  0.0 504.0 jit_solution(7329370030291426157)
XLA Ops:
  14.7 37.2 %all-reduce = bf16[3072]{0:T(1024)(128)(2,1)S(1)} all-reduce(bf16[3072]{0:T(1024)(128)(2,1)S(1)} %dynamic-update-slice), channel_id=1, replica_groups=mesh['ffn'=16,'tok'=2] {'ffn'}, use_global_device_ids=true, to_apply=%add | all-reduce | flops 3072 | bytes 12288
  53.2 4.5 fusion.22
  57.7 4.3 copy.57
  66.2 3.5 fusion
  69.7 3.7 exponential_reduce_fusion
  74.3 4.8 fusion.34
  82.1 13.0 %all-gather.4.cloned.1.call-done = bf16[2,3072,768]{2,1,0:T(8,128)(2,1)} async-done(((bf16[2,192,768]{2,1,0:T(8,128)(2,1)}), bf16[2,3072,768]{2,1,0:T(8,128)(2,1)}) %all-gather.4.cloned.1.call-update) | async-done | bytes 9437200 | tf_op jit(solution)/shard_map/all_gather | solution.py:126
  95.1 18.9 %fusion.5 = (bf16[512,3072]{1,0:T(8,128)(2,1)S(1)}, f32[512,3072]{1,0:T(8,128)S(1)}) fusion(f32[3072]{0:T(1024)} %fusion.45, f32[3072]{0:T(1024)S(1)} %copy-done.16, bf16[2,3072,768]{2,1,0:T(8,128)(2,1)} %all-gather.4.cloned.1.call-done, f32[512,768]{1,0:T(8,128)} %copy-done.6, f32[768]{0:T(1024)} %param.25, f32[768]{0:T(1024)} %param.24, ...), kind=kOutput, calls=%fused_computation.14 | convolution fusion | flops 2523267072 | bytes 15765504 | tf_op jit(solution)/shard_map/dot_general | solution.py:52
  121.2 4.4 fusion.21
  125.5 6.3 %convert_reduce_fusion = (f32[3072]{0:T(1024)}, bf16[512,3072]{1,0:T(8,128)(2,1)S(1)}) fusion(f32[3072]{0:T(1024)S(1)} %copy-done.17, f32[512,3072]{1,0:T(8,128)S(1)} %get-tuple-element.119, f32[3072]{0:T(1024)S(1)} %copy-done.16, bf16[2,3072,768]{2,1,0:T(8,128)(2,1)S(1)} %copy-done.28, f32[512,768]{1,0:T(8,128)S(1)} %get-tuple-element.93), kind=kOutput, calls=%fused_computation.22 | convolution fusion | flops 2438329344 | bytes 15765504 | tf_op jit(solution)/shard_map/dot_general | solution.py:52
  133.5 5.0 fusion.20
  138.6 8.2 %pad_maximum_fusion = bf16[2,3072,768]{2,1,0:T(8,128)(2,1)} fusion(bf16[1,3072,768]{2,1,0:T(8,128)(2,1)} %fusion.21, bf16[1,3072,768]{2,1,0:T(8,128)(2,1)} %fusion.20), kind=kLoop, calls=%fused_computation.9 | loop fusion | flops 4718592 | bytes 18874368 | tf_op jit(solution)/shard_map/stack | solution.py:152
  147.5 8.3 %multiply_reduce_fusion.1 = (f32[768]{0:T(1024)}, f32[512]{0:T(512)S(1)}, f32[512]{0:T(512)S(1)}, f32[768]{0:T(1024)}, f32[512,768]{1,0:T(8,128)S(1)}) fusion(f32[512,768]{1,0:T(8,128)} %copy-done.6, f32[512]{0:T(512)S(1)} %copy-done.20, f32[512]{0:T(512)S(1)} %broadcast_multiply_fusion.5, f32[768]{0:T(1024)S(1)} %copy-done.22, f32[512,768]{1,0:T(8,128)} %copy-done.11, ...), kind=kOutput, calls=%fused_computation.66 | convolution fusion | flops 2419848704 | bytes 12600320 | tf_op jit(solution)/shard_map/dot_general | solution.py:151
  162.2 14.8 %multiply_reduce_fusion = (f32[12,512]{1,0:T(8,128)S(1)}, f32[12,512,512]{1,2,0:T(8,128)}) fusion(f32[12,512,512]{1,2,0:T(8,128)} %copy-done.1, f32[12,512]{1,0:T(8,128)} %copy-done.13, pred[512,512]{0,1:T(8,128)(4,1)} %copy-done.3, bf16[1,512,3,12,64]{1,4,3,2,0:T(8,128)(2,1)} %bitcast.111, bf16[512,12,64]{0,2,1:T(8,128)(2,1)} %bitcast.114, ...), kind=kOutput, calls=%fused_computation.2 | convolution fusion | flops 418768896 | bytes 27058200 | tf_op jit(solution)/shard_map/rqhd,rkhd->rhqk/dot_general | solution.py:177
  177.1 7.7 %multiply_convert_fusion = bf16[12,512,512]{1,2,0:T(8,128)(2,1)S(1)} fusion(f32[12,512,512]{1,2,0:T(8,128)} %get-tuple-element.124, f32[12,512,512]{1,2,0:T(8,128)S(1)} %bitcast.108, f32[12,512]{1,0:T(8,128)S(1)} %get-tuple-element.123, f32[12,512]{1,0:T(8,128)S(1)} %copy-done.14, pred[512,512]{0,1:T(8,128)(4,1)S(1)} %copy-done.4), kind=kLoop, calls=%fused_computation.1 | loop fusion | flops 18874368 | bytes 31768576 | tf_op jit(solution)/shard_map/convert_element_type | solution.py:180
  188.0 3.7 convolution_bitcast_fusion
  206.0 3.5 convolution_convert_fusion.3
  209.4 5.7 %fusion.23 = bf16[768,2304]{0,1:T(8,128)(2,1)} fusion(bf16[512,2304]{0,1:T(8,128)(2,1)} %bitcast.116, bf16[512,768]{1,0:T(8,128)(2,1)} %param.18), kind=kOutput, calls=%fused_computation.49 | convolution fusion | flops 1813708800 | bytes 6684672 | tf_op jit(solution)/shard_map/dot_general | solution.py:46
  216.4 40.1 %reduce-scatter.2.cloned.1.call-done = bf16[2,192,768]{2,1,0:T(8,128)(2,1)} async-done(((bf16[2,3072,768]{2,1,0:T(8,128)(2,1)}), bf16[2,192,768]{2,1,0:T(8,128)(2,1)}) %reduce-scatter.2.cloned.1.call-update) | async-done | bytes 589840 | tf_op jit(solution)/shard_map/reduce_scatter | solution.py:155
  256.5 5.3 %convolution_add_fusion.1 = f32[512,768]{1,0:T(8,128)} fusion(f32[512,768]{1,0:T(8,128)} %copy-done.5, bf16[512,2304]{0,1:T(8,128)(2,1)} %bitcast.117, bf16[768,2304]{1,0:T(8,128)(2,1)S(1)} %copy-done), kind=kOutput, calls=%fused_computation.83 | convolution fusion | flops 1812332544 | bytes 9043968 | tf_op jit(solution)/shard_map/dot_general | solution.py:52
  265.1 48.6 %all-gather.6.cloned.1.call-done = f32[294912]{0:T(1024)} async-done(((f32[9216]{0:T(1024)}), f32[294912]{0:T(1024)}) %all-gather.6.cloned.1.call-update) | async-done | bytes 1179664 | tf_op jit(solution)/shard_map/all_gather | solution.py:13
  320.9 143.0 %all-reduce.7.cloned.1.call-done = (bf16[768,2304]{0,1:T(8,128)(2,1)}, bf16[768,768]{1,0:T(8,128)(2,1)}) async-done(((bf16[768,2304]{0,1:T(8,128)(2,1)}, bf16[768,768]{1,0:T(8,128)(2,1)}), (bf16[768,2304]{0,1:T(8,128)(2,1)}, bf16[768,768]{1,0:T(8,128)(2,1)})) %all-reduce.7.cloned.1.call-update) | async-done | bytes 4718608 | tf_op jit(solution)/shard_map/psum | solution.py:201
  466.8 5.9 %copy.63 = f32[768,2304]{1,0:T(8,128)} copy(bf16[768,2304]{0,1:T(8,128)(2,1)} %get-tuple-element.90) | data formatting | bytes 10616832
  472.8 22.2 %all-reduce.5.cloned.1.call-done = bf16[2,192,768]{2,1,0:T(8,128)(2,1)} async-done(((bf16[2,192,768]{2,1,0:T(8,128)(2,1)}), bf16[2,192,768]{2,1,0:T(8,128)(2,1)}) %all-reduce.5.cloned.1.call-update) | async-done | bytes 589840 | tf_op jit(solution)/shard_map/psum | solution.py:156
  (148 shorter events, 66.0 us)
Async XLA Ops:
  7.2 46.0 %copy-start = (bf16[768,2304]{1,0:T(8,128)(2,1)S(1)}, bf16[768,2304]{1,0:T(8,128)(2,1)}, u32[]{:S(2)}) copy-start(bf16[768,2304]{1,0:T(8,128)(2,1)} %param.19) | copy-start | bytes 10616836
  7.2 87.9 %all-gather.4.cloned.1.call-start = ((), (), s32[]{:S(2)}) async-start(), calls=%async_computation.1 | async-start | bytes 10027008 | tf_op jit(solution)/shard_map/all_gather | solution.py:126
  9.3 247.2 %reduce-scatter.2.cloned.1.call-start = ((), (), s32[]{:S(2)}) async-start(), calls=%async_computation.2 | async-start | bytes 10027008 | tf_op jit(solution)/shard_map/reduce_scatter | solution.py:155
  57.7 8.2 %copy-start.18 = (s32[512]{0:T(512)S(1)}, s32[512]{0:T(512)}, u32[]{:S(2)}) copy-start(s32[512]{0:T(512)} %param.32) | copy-start | bytes 6148
  73.4 5.6 %copy-start.13 = (f32[12,512]{1,0:T(8,128)}, f32[12,512]{1,0:T(8,128)S(1)}, u32[]{:S(2)}) copy-start(f32[12,512]{1,0:T(8,128)S(1)} %log_add_fusion) | copy-start | bytes 73732
  74.3 4.8 copy-start.31
  79.1 16.0 %copy-start.16 = (f32[3072]{0:T(1024)S(1)}, f32[3072]{0:T(1024)}, u32[]{:S(2)}) copy-start(f32[3072]{0:T(1024)} %convert_element_type.154) | copy-start | bytes 36868
  95.1 18.9 %copy-start.7 = (f32[512,768]{1,0:T(8,128)S(1)}, f32[512,768]{1,0:T(8,128)}, u32[]{:S(2)}) copy-start(f32[512,768]{1,0:T(8,128)} %copy-done.6) | copy-start | bytes 4718596
  95.1 18.9 %copy-start.19 = (f32[512]{0:T(512)S(1)}, f32[512]{0:T(512)}, u32[]{:S(2)}) copy-start(f32[512]{0:T(512)} %add_rsqrt_fusion.1) | copy-start | bytes 6148
  95.1 18.9 %copy-start.21 = (f32[768]{0:T(1024)S(1)}, f32[768]{0:T(1024)}, u32[]{:S(2)}) copy-start(f32[768]{0:T(1024)} %param.24) | copy-start | bytes 9220
  95.1 18.9 %copy-start.23 = (f32[768]{0:T(1024)S(1)}, f32[768]{0:T(1024)}, u32[]{:S(2)}) copy-start(f32[768]{0:T(1024)} %convert_element_type.157) | copy-start | bytes 9220
  95.1 18.9 %copy-start.28 = (bf16[2,3072,768]{2,1,0:T(8,128)(2,1)S(1)}, bf16[2,3072,768]{2,1,0:T(8,128)(2,1)}, u32[]{:S(2)}) copy-start(bf16[2,3072,768]{2,1,0:T(8,128)(2,1)} %all-gather.4.cloned.1.call-done) | copy-start | bytes 28311556
  95.1 18.9 %copy-start.32 = (f32[768]{0:T(1024)S(1)}, f32[768]{0:T(1024)}, u32[]{:S(2)}) copy-start(f32[768]{0:T(1024)} %param.25) | copy-start | bytes 9220
  146.8 166.9 %all-gather.6.cloned.1.call-start = ((), (), s32[]{:S(2)}) async-start(), calls=%async_computation.4 | async-start | bytes 1216512 | tf_op jit(solution)/shard_map/all_gather | solution.py:13
  147.5 8.3 %copy-start.8 = (f32[512,768]{1,0:T(8,128)S(1)}, f32[512,768]{1,0:T(8,128)}, u32[]{:S(2)}) copy-start(f32[512,768]{1,0:T(8,128)} %copy-done.6) | copy-start | bytes 4718596
  155.8 6.4 %copy-start.27 = (bf16[12]{0:T(256)(128)(2,1)S(1)}, bf16[12]{0:T(256)(128)(2,1)}, u32[]{:S(2)}) copy-start(bf16[12]{0:T(256)(128)(2,1)} %get-tuple-element.128) | copy-start | bytes 76
  162.1 14.9 %slice-start = ((s8[12582912]{0:T(1024)(128)(4,1)}), s8[4194304]{0:T(1024)(128)(4,1)S(1)}, s32[]{:S(2)}) async-start(s8[12582912]{0:T(1024)(128)(4,1)} %bitcast.107), calls=%async_computation.6 | async-start | bytes 8388608
  162.1 14.9 %slice-start.1 = ((s8[12582912]{0:T(1024)(128)(4,1)}), s8[4194304]{0:T(1024)(128)(4,1)S(1)}, s32[]{:S(2)}) async-start(s8[12582912]{0:T(1024)(128)(4,1)} %bitcast.107), calls=%async_computation.7 | async-start | bytes 8388608
  162.1 14.9 %slice-start.2 = ((s8[12582912]{0:T(1024)(128)(4,1)}), s8[4194304]{0:T(1024)(128)(4,1)S(1)}, s32[]{:S(2)}) async-start(s8[12582912]{0:T(1024)(128)(4,1)} %bitcast.107), calls=%async_computation.8 | async-start | bytes 8388608
  162.1 14.9 %copy-start.4 = (pred[512,512]{0,1:T(8,128)(4,1)S(1)}, pred[512,512]{0,1:T(8,128)(4,1)}, u32[]{:S(2)}) copy-start(pred[512,512]{0,1:T(8,128)(4,1)} %copy-done.3) | copy-start | bytes 786436
  162.2 14.9 %copy-start.14 = (f32[12,512]{1,0:T(8,128)S(1)}, f32[12,512]{1,0:T(8,128)}, u32[]{:S(2)}) copy-start(f32[12,512]{1,0:T(8,128)} %copy-done.13) | copy-start | bytes 73732
  177.0 7.8 %copy-start.2 = (bf16[512,2304]{0,1:T(8,128)(2,1)S(1)}, bf16[512,2304]{0,1:T(8,128)(2,1)}, u32[]{:S(2)}) copy-start(bf16[512,2304]{0,1:T(8,128)(2,1)} %copy.57) | copy-start | bytes 7077892
  205.9 258.0 %all-reduce.7.cloned.1.call-start = ((), (), s32[]{:S(2)}) async-start(), calls=%async_computation.5 | async-start | bytes 9437184 | tf_op jit(solution)/shard_map/psum | solution.py:201
  215.2 279.8 %all-reduce.5.cloned.1.call-start = ((), (), s32[]{:S(2)}) async-start(), calls=%async_computation.3 | async-start | bytes 1179648 | tf_op jit(solution)/shard_map/psum | solution.py:156
  (19 other events, 53.3 us)
Sparse Core Ops, SparseCore 0:
  10.9 84.1 all-gather.3
  146.9 109.5 reduce-scatter.1
  260.0 53.6 all-gather.5
  320.0 143.9 all-reduce.6
  466.1 28.8 all-reduce.4
